TPU v7x, 32 devices: a whole 2x2x4 slice. The times are simulated.
32 devices in a mesh: dp: 16 (over z, x, core), tensor: 2 (over y).
Axes of the slice: x: 2, y: 2, z: 4, core: 2. Of those that a mesh axis runs over, the one named last changes fastest.
Arguments:
- tokens: bfloat16 [8192, 2048], P('dp'), may hold values from -6 to 6
- segments: int32 [16, 512], P('dp'), may hold values from 0 to 3, never falling along the last dimension, each value on 1 to 384 neighbouring positions
- cotangent: bfloat16 [8192, 2048], P('dp'), may hold values from -6 to 6
- norm_gain: float32 [2048], P('dp'), may hold values from 0.1 to 1.9
- attn_weight: float32 [2048, 4, 2048], P('dp', None, 'tensor'), may hold values from -0.125 to 0.125
- beta_weight: float32 [2048, 16], P('dp', 'tensor'), may hold values from -0.125 to 0.125
- conv_weight: float32 [3, 4, 16, 128], P(None, None, 'tensor', 'dp'), may hold values from -3 to 3
- out_gain: float32 [128], P('dp'), may hold values from 0.1 to 1.9
- mlp_gain: float32 [2048], P('dp'), may hold values from 0.1 to 1.9
- mlp_weight: float32 [2048, 3, 5632], P('dp', None, 'tensor'), may hold values from -0.125 to 0.125
Outputs:
- output: bfloat16 [8192, 2048], P('dp')
- input_grad: float32 [8192, 2048], P('dp')
- norm_gain_grad: float32 [2048], P('dp')
- attn_weight_grad: float32 [2048, 4, 2048], P('dp', None, 'tensor')
- beta_weight_grad: float32 [2048, 16], P('dp', 'tensor')
- conv_weight_grad: float32 [3, 4, 16, 128], P(None, None, 'tensor', 'dp')
- out_gain_grad: float32 [128], P('dp')
- mlp_gain_grad: float32 [2048], P('dp')
- mlp_weight_grad: float32 [2048, 3, 5632], P('dp', None, 'tensor')
Inputs may be any that keep to these rules, and one draw needn't show every extreme that they name: `segments`: within a sequence the numbers never fall; a document (a run of one number) has 1 to 384 tokens, and some document has exactly 384.
All inputs are finite; a program needn't handle non-finite values.
Results may differ from a plain program's by a relative error of at most 0.017.
The roundings to bfloat16 on the way count: a program that leaves them out, or rounds other values in their place, can miss the bound.
Values may be sent and summed in bfloat16 or wider, within the bound.
No kernel may reach another device: no remote copies, remote signals or barrier semaphores. Data moves between devices by JAX's collectives and lax.ppermute only.
A program may use at most 384 MiB of HBM per device.

v0:
```python
import jax
import jax.numpy as jnp
from jax import lax
from jax.sharding import PartitionSpec as P

BLOCK = 64
highest = lax.Precision.HIGHEST


def rms_scale(values, gain_values, epsilon):
    return (
        values
        * lax.rsqrt(jnp.mean(values * values, axis=-1, keepdims=True) + epsilon)
        * gain_values
    )


def norm_apply(values, gain_values):
    return rms_scale(values, gain_values, 1e-05)


def short_conv(signal, weight, seg_ids):
    length = signal.shape[0]
    summed = signal * weight[3]
    for offset in range(1, 4):
        pad_rows = jnp.zeros((offset,) + signal.shape[1:], signal.dtype)
        shifted = jnp.concatenate([pad_rows, signal[: length - offset]], axis=0)
        prior_ids = jnp.concatenate(
            [jnp.full((offset,), -1, jnp.int32), seg_ids[: length - offset]], axis=0
        )
        allowed = (prior_ids == seg_ids).astype(signal.dtype)
        summed = summed + shifted * allowed[:, None, None] * weight[3 - offset]
    return summed


def delta_block(memory, inputs):
    queries, key_vecs, values, strength, seg_ids, prior_id = inputs
    block_len = seg_ids.shape[0]
    carry_in = (seg_ids == prior_id).astype(queries.dtype)
    same_doc = (seg_ids[:, None] == seg_ids[None, :]).astype(queries.dtype)
    row_ids = jnp.arange(block_len)
    strict = (row_ids[:, None] > row_ids[None, :]).astype(queries.dtype)
    causal = (row_ids[:, None] >= row_ids[None, :]).astype(queries.dtype)
    key_inner = jnp.einsum("ihd,jhd->hij", key_vecs, key_vecs, precision=highest) * (
        same_doc * strict
    )
    weights_t = jnp.transpose(strength)
    system = jnp.eye(block_len, dtype=queries.dtype) + weights_t[:, :, None] * key_inner
    recalled = jnp.einsum("hvd,ihd->hiv", memory, key_vecs, precision=highest)
    target = weights_t[:, :, None] * (
        jnp.transpose(values, (1, 0, 2)) - carry_in[None, :, None] * recalled
    )
    writes = lax.linalg.triangular_solve(
        system, target, left_side=True, lower=True, unit_diagonal=True
    )
    scores = jnp.einsum("ihd,jhd->hij", queries, key_vecs, precision=highest) * (same_doc * causal)
    carried = jnp.einsum("hvd,ihd->hiv", memory, queries, precision=highest)
    output = carry_in[None, :, None] * carried + jnp.einsum(
        "hij,hjv->hiv", scores, writes, precision=highest
    )
    final_doc = same_doc[block_len - 1]
    updated = carry_in[block_len - 1] * memory + jnp.einsum(
        "hjv,jhd->hvd", writes * final_doc[None, :, None], key_vecs, precision=highest
    )
    return (updated, jnp.transpose(output, (1, 0, 2)))


def delta_sequence(queries, key_vecs, values, strength, seg_ids):
    length = queries.shape[0]
    head_count = queries.shape[1]
    head_width = queries.shape[2]
    block_count = length // BLOCK
    prior_ids = jnp.concatenate(
        [jnp.full((1,), -1, jnp.int32), seg_ids[BLOCK - 1 : length - 1 : BLOCK]], axis=0
    )

    def blocked(array_in):
        return array_in.reshape((block_count, BLOCK) + array_in.shape[1:])

    initial = jnp.zeros((head_count, head_width, head_width), queries.dtype)
    final_state, outputs = lax.scan(
        jax.checkpoint(delta_block),
        initial,
        (
            blocked(queries),
            blocked(key_vecs),
            blocked(values),
            blocked(strength),
            blocked(seg_ids),
            prior_ids,
        ),
    )
    return outputs.reshape(queries.shape)


def token_mixer(projected, beta_logits, conv_weight, out_gain, seg_ids):
    length = projected.shape[0]
    convolved = [
        jax.nn.silu(short_conv(projected[:, which], conv_weight[which], seg_ids))
        for which in range(3)
    ]
    queries = convolved[0] * lax.rsqrt(
        jnp.sum(convolved[0] * convolved[0], axis=-1, keepdims=True) + 1e-06
    )
    key_vecs = convolved[1] * lax.rsqrt(
        jnp.sum(convolved[1] * convolved[1], axis=-1, keepdims=True) + 1e-06
    )
    strength = jax.nn.sigmoid(beta_logits)
    output = delta_sequence(queries, key_vecs, convolved[2], strength, seg_ids)
    return rms_scale(output, out_gain, 1e-05).reshape(length, -1)


def body(
    tokens,
    segments,
    cotangent,
    norm_gain,
    attn_weight,
    beta_weight,
    conv_weight,
    out_gain,
    mlp_gain,
    mlp_weight,
):
    seg_ids = segments[0]
    length = tokens.shape[0]
    gain_in_low = norm_gain.astype(jnp.bfloat16)
    attn_low = attn_weight.astype(jnp.bfloat16)
    beta_low = beta_weight.astype(jnp.bfloat16)
    gain_mid_low = mlp_gain.astype(jnp.bfloat16)
    mlp_low = mlp_weight.astype(jnp.bfloat16)
    gain_in, attn_mat, beta_mat, conv_full, gain_heads = (
        lax.all_gather(gain_in_low, "dp", axis=0, tiled=True),
        lax.all_gather(attn_low, "dp", axis=0, tiled=True),
        lax.all_gather(beta_low, "dp", axis=0, tiled=True),
        lax.all_gather(conv_weight.astype(jnp.bfloat16), "dp", axis=3, tiled=True),
        lax.all_gather(out_gain.astype(jnp.bfloat16), "dp", axis=0, tiled=True),
    )
    gain_mid, mlp_mat = (
        lax.all_gather(gain_mid_low, "dp", axis=0, tiled=True),
        lax.all_gather(mlp_low, "dp", axis=0, tiled=True),
    )
    model_width = attn_mat.shape[0]
    local_width = attn_mat.shape[2]
    head_count = conv_full.shape[2]
    head_width = conv_full.shape[3]
    inputs_f = tokens.astype(jnp.float32)
    normed = rms_scale(inputs_f, gain_in.astype(jnp.float32), 1e-05).astype(jnp.bfloat16)
    qkv_mat = attn_mat[:, :3].reshape(model_width, 3 * local_width)
    projected = jnp.dot(normed, qkv_mat, preferred_element_type=jnp.float32)
    beta_logits = jnp.dot(normed, beta_mat, preferred_element_type=jnp.float32)

    def local_mixer(proj_value, logit_value, conv_value, heads_gain):
        return token_mixer(
            proj_value.reshape(length, 3, head_count, head_width),
            logit_value,
            conv_value,
            heads_gain,
            seg_ids,
        )

    mixed, mixer_pull = jax.vjp(
        local_mixer,
        projected,
        beta_logits,
        conv_full.astype(jnp.float32),
        gain_heads.astype(jnp.float32),
    )
    mixed_low = mixed.astype(jnp.bfloat16)
    attn_part = jnp.einsum(
        "tc,oc->to", mixed_low, attn_mat[:, 3], preferred_element_type=jnp.float32
    )
    attended = lax.psum(attn_part, "tensor")
    hidden = inputs_f + attended
    normed_mlp = rms_scale(hidden, gain_mid.astype(jnp.float32), 1e-05).astype(jnp.bfloat16)
    gate_up = jnp.einsum(
        "td,dgf->tgf", normed_mlp, mlp_mat[:, :2], preferred_element_type=jnp.float32
    )
    gate_vals = gate_up[:, 0]
    up_vals = gate_up[:, 1]
    activated = (jax.nn.silu(gate_vals) * up_vals).astype(jnp.bfloat16)
    down_part = jnp.einsum(
        "tf,of->to", activated, mlp_mat[:, 2], preferred_element_type=jnp.float32
    )
    mlp_out = lax.psum(down_part.astype(jnp.bfloat16), "tensor").astype(jnp.float32)
    result = (hidden + mlp_out).astype(jnp.bfloat16)
    gain_in, attn_mat, beta_mat = (
        lax.all_gather(gain_in_low, "dp", axis=0, tiled=True),
        lax.all_gather(attn_low, "dp", axis=0, tiled=True),
        lax.all_gather(beta_low, "dp", axis=0, tiled=True),
    )
    gain_mid, mlp_mat = (
        lax.all_gather(gain_mid_low, "dp", axis=0, tiled=True),
        lax.all_gather(mlp_low, "dp", axis=0, tiled=True),
    )
    grad_act = jnp.einsum("to,of->tf", cotangent, mlp_mat[:, 2], preferred_element_type=jnp.float32)
    gate_sig = jax.nn.sigmoid(gate_vals)
    grad_gate = grad_act * up_vals * gate_sig * (1.0 + gate_vals * (1.0 - gate_sig))
    grad_up = grad_act * gate_vals * gate_sig
    grad_gate_up = jnp.stack([grad_gate, grad_up], axis=1).astype(jnp.bfloat16)
    normed_rows = normed_mlp
    grad_rows = cotangent
    first_part = jnp.einsum(
        "tc,tgf->cgf", normed_rows, grad_gate_up, preferred_element_type=jnp.float32
    )
    last_part = jnp.einsum("tc,tf->cf", grad_rows, activated, preferred_element_type=jnp.float32)
    mlp_grad = lax.psum_scatter(
        jnp.concatenate([first_part, last_part[:, None]], axis=1),
        "dp",
        scatter_dimension=0,
        tiled=True,
    )
    grad_normed_mlp_part = jnp.einsum(
        "tgf,dgf->td", grad_gate_up, mlp_mat[:, :2], preferred_element_type=jnp.float32
    )
    grad_normed_mlp = lax.psum(grad_normed_mlp_part.astype(jnp.bfloat16), "tensor").astype(
        jnp.float32
    )
    normed_again, mid_pull = jax.vjp(norm_apply, hidden, gain_mid.astype(jnp.float32))
    grad_hidden_norm, grad_gain_mid = mid_pull(grad_normed_mlp)
    grad_hidden = cotangent.astype(jnp.float32) + grad_hidden_norm
    grad_hidden_low = grad_hidden.astype(jnp.bfloat16)
    grad_mixed = jnp.einsum(
        "to,oc->tc", grad_hidden_low, attn_mat[:, 3], preferred_element_type=jnp.float32
    )
    grad_proj, grad_logits, grad_conv, grad_gain_heads = mixer_pull(grad_mixed)
    grad_proj_low = grad_proj.reshape(length, 3, local_width).astype(jnp.bfloat16)
    grad_logits_low = grad_logits.astype(jnp.bfloat16)
    normed_rows = normed
    grad_rows = grad_hidden_low
    first_part = jnp.einsum(
        "tc,tpe->cpe", normed_rows, grad_proj_low, preferred_element_type=jnp.float32
    )
    last_part = jnp.einsum("tc,te->ce", grad_rows, mixed_low, preferred_element_type=jnp.float32)
    attn_grad = lax.psum_scatter(
        jnp.concatenate([first_part, last_part[:, None]], axis=1),
        "dp",
        scatter_dimension=0,
        tiled=True,
    )
    grad_beta = jnp.einsum("td,th->dh", normed, grad_logits_low, preferred_element_type=jnp.float32)
    grad_normed_part = jnp.einsum(
        "tpe,dpe->td", grad_proj_low, attn_mat[:, :3], preferred_element_type=jnp.float32
    )
    grad_normed_part = grad_normed_part + jnp.einsum(
        "th,dh->td", grad_logits_low, beta_mat, preferred_element_type=jnp.float32
    )
    grad_normed, grad_gain_heads = (
        lax.psum(grad_normed_part.astype(jnp.bfloat16), "tensor").astype(jnp.float32),
        lax.psum(grad_gain_heads.astype(jnp.bfloat16), "tensor").astype(jnp.float32),
    )
    normed_first, in_pull = jax.vjp(norm_apply, inputs_f, gain_in.astype(jnp.float32))
    grad_inputs_norm, grad_gain_in = in_pull(grad_normed)
    grad_inputs = grad_hidden + grad_inputs_norm
    small_sums = (
        lax.psum_scatter(grad_gain_in, "dp", scatter_dimension=0, tiled=True),
        lax.psum_scatter(grad_beta, "dp", scatter_dimension=0, tiled=True),
        lax.psum_scatter(grad_conv, "dp", scatter_dimension=3, tiled=True),
        lax.psum_scatter(grad_gain_heads, "dp", scatter_dimension=0, tiled=True),
        lax.psum_scatter(grad_gain_mid, "dp", scatter_dimension=0, tiled=True),
    )
    return (
        result,
        grad_inputs,
        small_sums[0],
        attn_grad,
        small_sums[1],
        small_sums[2],
        small_sums[3],
        small_sums[4],
        mlp_grad,
    )


def solution(mesh):
    return jax.shard_map(
        body,
        mesh=mesh,
        in_specs=(
            P("dp", None),
            P("dp", None),
            P("dp", None),
            P("dp"),
            P("dp", None, "tensor"),
            P("dp", "tensor"),
            P(None, None, "tensor", "dp"),
            P("dp"),
            P("dp"),
            P("dp", None, "tensor"),
        ),
        out_specs=(
            P("dp", None),
            P("dp", None),
            P("dp"),
            P("dp", None, "tensor"),
            P("dp", "tensor"),
            P(None, None, "tensor", "dp"),
            P("dp"),
            P("dp"),
            P("dp", None, "tensor"),
        ),
        check_vma=False,
    )
```

profile of v0, /device:TPU:0, one launch (start us, length us, event | category | flops | bytes accessed | tf_op | source)
XLA Modules:
  0.0 2766.3 jit_solution(18114808187447301338)
XLA Ops:
  201.9 432.9 %while.38 = (s32[]{:T(128)}, f32[8,128,128]{2,1,0:T(8,128)S(1)}, f32[8,64,8,128]{3,1,2,0:T(8,128)}, f32[8,8,128,128]{3,2,1,0:T(8,128)}, s32[8,64]{1,0:T(8,128)S(...) while((s32[]{:T(128)}, f32[8,128,128]{2,1,0:T(8,128)S(1)}, ...), condition=%wide.region_4.6_spmd.clone, body=%wide.region_3.5_spmd.clone.sunk | while | flops 504746240 | bytes 7759869 | solution.py:81
  205.8 39.3 %custom-call.24 = f32[8,1,64,64]{2,3,1,0:T(8,128)S(1)} custom-call(f32[8,1,64,64]{3,2,1,0:T(8,128)S(1)} %fusion.307), custom_call_target="InvertDiagBlocksLowerTriangular" | custom-call | tf_op jit(solution)/shard_map/jvp()/while/body/eval_jaxpr/triangular_solve/custom-call.1 | solution.py:53
  259.9 39.3 %custom-call.24 = f32[8,1,64,64]{2,3,1,0:T(8,128)S(1)} custom-call(f32[8,1,64,64]{3,2,1,0:T(8,128)S(1)} %fusion.307), custom_call_target="InvertDiagBlocksLowerTriangular" | custom-call | tf_op jit(solution)/shard_map/jvp()/while/body/eval_jaxpr/triangular_solve/custom-call.1 | solution.py:53
  314.0 39.3 %custom-call.24 = f32[8,1,64,64]{2,3,1,0:T(8,128)S(1)} custom-call(f32[8,1,64,64]{3,2,1,0:T(8,128)S(1)} %fusion.307), custom_call_target="InvertDiagBlocksLowerTriangular" | custom-call | tf_op jit(solution)/shard_map/jvp()/while/body/eval_jaxpr/triangular_solve/custom-call.1 | solution.py:53
  368.1 39.3 %custom-call.24 = f32[8,1,64,64]{2,3,1,0:T(8,128)S(1)} custom-call(f32[8,1,64,64]{3,2,1,0:T(8,128)S(1)} %fusion.307), custom_call_target="InvertDiagBlocksLowerTriangular" | custom-call | tf_op jit(solution)/shard_map/jvp()/while/body/eval_jaxpr/triangular_solve/custom-call.1 | solution.py:53
  422.2 39.3 %custom-call.24 = f32[8,1,64,64]{2,3,1,0:T(8,128)S(1)} custom-call(f32[8,1,64,64]{3,2,1,0:T(8,128)S(1)} %fusion.307), custom_call_target="InvertDiagBlocksLowerTriangular" | custom-call | tf_op jit(solution)/shard_map/jvp()/while/body/eval_jaxpr/triangular_solve/custom-call.1 | solution.py:53
  476.3 39.3 %custom-call.24 = f32[8,1,64,64]{2,3,1,0:T(8,128)S(1)} custom-call(f32[8,1,64,64]{3,2,1,0:T(8,128)S(1)} %fusion.307), custom_call_target="InvertDiagBlocksLowerTriangular" | custom-call | tf_op jit(solution)/shard_map/jvp()/while/body/eval_jaxpr/triangular_solve/custom-call.1 | solution.py:53
  530.4 39.3 %custom-call.24 = f32[8,1,64,64]{2,3,1,0:T(8,128)S(1)} custom-call(f32[8,1,64,64]{3,2,1,0:T(8,128)S(1)} %fusion.307), custom_call_target="InvertDiagBlocksLowerTriangular" | custom-call | tf_op jit(solution)/shard_map/jvp()/while/body/eval_jaxpr/triangular_solve/custom-call.1 | solution.py:53
  584.5 39.3 %custom-call.24 = f32[8,1,64,64]{2,3,1,0:T(8,128)S(1)} custom-call(f32[8,1,64,64]{3,2,1,0:T(8,128)S(1)} %fusion.307), custom_call_target="InvertDiagBlocksLowerTriangular" | custom-call | tf_op jit(solution)/shard_map/jvp()/while/body/eval_jaxpr/triangular_solve/custom-call.1 | solution.py:53
  684.3 67.2 %all-reduce.50.cloned.1.call-done = f32[512,2048]{1,0:T(8,128)} async-done(((f32[512,2048]{1,0:T(8,128)}), f32[512,2048]{1,0:T(8,128)}) %all-reduce.50.cloned.1.call-update) | async-done | bytes 4194320 | tf_op jit(solution)/shard_map/psum | solution.py:173
  756.2 170.0 %all-gather.7.cloned.1.call-done = bf16[2048,3,2816]{2,0,1:T(8,128)(2,1)} async-done(((bf16[128,3,2816]{2,0,1:T(8,128)(2,1)}), bf16[2048,3,2816]{2,0,1:T(8,128)(2,1)}) %all-gather.7.cloned.1.call-update) | async-done | bytes 34603024 | tf_op jit(solution)/shard_map/all_gather | solution.py:141
  996.0 47.1 %all-reduce.52.cloned.1.call-done = bf16[512,2048]{1,0:T(8,128)(2,1)} async-done(((bf16[512,2048]{1,0:T(8,128)(2,1)}), bf16[512,2048]{1,0:T(8,128)(2,1)}) %all-reduce.52.cloned.1.call-update) | async-done | bytes 2097168 | tf_op jit(solution)/shard_map/psum | solution.py:216
  1062.7 495.5 %while.39 = (s32[]{:T(128)}, f32[8,128,128]{2,1,0:T(8,128)S(1)}, f32[8,64,8,128]{3,1,0,2:T(8,128)}, f32[8,64,8,128]{3,1,0,2:T(8,128)}, f32[8,64,8,128]{3,1,0,2:T...) while((s32[]{:T(128)}, f32[8,128,128]{2,1,0:T(8,128)S(1)}, ...), condition=%wide.region_15.17_spmd.clone, body=%wide.region_12.16_spmd.clone.sunk | while | flops 1285967616 | bytes 23183872 | solution.py:81
  1071.0 39.3 %custom-call.25 = f32[8,1,64,64]{2,3,1,0:T(8,128)S(1)} custom-call(f32[8,1,64,64]{3,2,1,0:T(8,128)S(1)} %add_bitcast_fusion.8), custom_call_target="InvertDiagBlocksLowerTriangular" | custom-call | tf_op jit(solution)/shard_map/transpose(jvp())/while/body/eval_jaxpr/checkpoint/triangular_solve | solution.py:53
  1132.9 39.3 %custom-call.25 = f32[8,1,64,64]{2,3,1,0:T(8,128)S(1)} custom-call(f32[8,1,64,64]{3,2,1,0:T(8,128)S(1)} %add_bitcast_fusion.8), custom_call_target="InvertDiagBlocksLowerTriangular" | custom-call | tf_op jit(solution)/shard_map/transpose(jvp())/while/body/eval_jaxpr/checkpoint/triangular_solve | solution.py:53
  1194.8 39.3 %custom-call.25 = f32[8,1,64,64]{2,3,1,0:T(8,128)S(1)} custom-call(f32[8,1,64,64]{3,2,1,0:T(8,128)S(1)} %add_bitcast_fusion.8), custom_call_target="InvertDiagBlocksLowerTriangular" | custom-call | tf_op jit(solution)/shard_map/transpose(jvp())/while/body/eval_jaxpr/checkpoint/triangular_solve | solution.py:53
  1256.7 39.3 %custom-call.25 = f32[8,1,64,64]{2,3,1,0:T(8,128)S(1)} custom-call(f32[8,1,64,64]{3,2,1,0:T(8,128)S(1)} %add_bitcast_fusion.8), custom_call_target="InvertDiagBlocksLowerTriangular" | custom-call | tf_op jit(solution)/shard_map/transpose(jvp())/while/body/eval_jaxpr/checkpoint/triangular_solve | solution.py:53
  1318.6 39.3 %custom-call.25 = f32[8,1,64,64]{2,3,1,0:T(8,128)S(1)} custom-call(f32[8,1,64,64]{3,2,1,0:T(8,128)S(1)} %add_bitcast_fusion.8), custom_call_target="InvertDiagBlocksLowerTriangular" | custom-call | tf_op jit(solution)/shard_map/transpose(jvp())/while/body/eval_jaxpr/checkpoint/triangular_solve | solution.py:53
  1380.4 39.3 %custom-call.25 = f32[8,1,64,64]{2,3,1,0:T(8,128)S(1)} custom-call(f32[8,1,64,64]{3,2,1,0:T(8,128)S(1)} %add_bitcast_fusion.8), custom_call_target="InvertDiagBlocksLowerTriangular" | custom-call | tf_op jit(solution)/shard_map/transpose(jvp())/while/body/eval_jaxpr/checkpoint/triangular_solve | solution.py:53
  1686.4 49.2 %pad_maximum_fusion = f32[2048,3,2816]{2,0,1:T(8,128)} fusion(f32[2048,1,2816]{2,0,1:T(8,128)} %convolution_bitcast_fusion.5, f32[2048,2,2816]{2,0,1:T(8,128)} %fusion.116), kind=kLoop, calls=%fused_computation.142 | loop fusion | flops 17301504 | bytes 138412032 | tf_op jit(solution)/shard_map/concatenate | solution.py:208
  1746.1 63.7 %all-reduce.55 = (f32[2048]{0:T(1024)S(1)}, f32[3,4,8,128]{3,2,1,0:T(8,128)S(1)}, f32[128]{0:T(128)S(1)}, f32[2048]{0:T(1024)S(1)}) all-reduce(f32[2048]{0:T(1024)S(1)} %get-tuple-element.569, f32[3,4,8,128]{3,2,1,0:T(8,128)S(1)} %pad_add_fusion, bf16[128]{0:T(256)(128)(2,1)S(1)} %psum.39, ...), channel_id=2, replica_groups=mesh['dp'=16,'tensor'=2] {'dp'}, use_global_device_ids=true, to_apply=%region_21.23.clone | all-reduce | flops 16512 | bytes 131840
  1820.5 224.0 %reduce-scatter.5.cloned.1.call-done = f32[128,4,1024]{2,0,1:T(8,128)} async-done(((f32[2048,4,1024]{2,0,1:T(8,128)}), f32[128,4,1024]{2,0,1:T(8,128)}) %reduce-scatter.5.cloned.1.call-update) | async-done | bytes 2097168 | tf_op jit(solution)/shard_map/reduce_scatter | solution.py:235
  2048.7 51.1 %reduce-scatter.7.cloned.1.call-done = f32[128,8]{0,1:T(8,128)} async-done(((f32[2048,8]{0,1:T(8,128)}), f32[128,8]{0,1:T(8,128)}) %reduce-scatter.7.cloned.1.call-update) | async-done | bytes 4112 | tf_op jit(solution)/shard_map/reduce_scatter | solution.py:257
  2099.8 659.4 %reduce-scatter.9.cloned.1.call-done = f32[128,3,2816]{2,0,1:T(8,128)} async-done(((f32[2048,3,2816]{2,0,1:T(8,128)}), f32[128,3,2816]{2,0,1:T(8,128)}) %reduce-scatter.9.cloned.1.call-update) | async-done | bytes 4325392 | tf_op jit(solution)/shard_map/reduce_scatter | solution.py:207
  (817 shorter events, 863.4 us)
Async XLA Ops:
  7.3 138.2 %all-gather.5.cloned.1.call-start = ((), (), s32[]{:S(2)}) async-start(), calls=%async_computation.3 | async-start | bytes 17825792 | tf_op jit(solution)/shard_map/all_gather | solution.py:134
  11.2 740.4 %all-reduce.50.cloned.1.call-start = ((), (), s32[]{:S(2)}) async-start(), calls=%async_computation.4 | async-start | bytes 8388608 | tf_op jit(solution)/shard_map/psum | solution.py:173
  67.3 105.6 %copy-start.39 = (f32[16,1,128]{2,1,0:T(1,128)}, f32[16,1,128]{2,1,0:T(1,128)S(1)}, u32[]{:S(2)}) copy-start(f32[16,1,128]{2,1,0:T(1,128)S(1)} %convert_element_type.232) | copy-start | bytes 24580
  87.8 85.2 %copy-start.78 = (f32[512]{0:T(512)}, f32[512]{0:T(512)S(1)}, u32[]{:S(2)}) copy-start(f32[512]{0:T(512)S(1)} %fusion.174) | copy-start | bytes 6148
  110.8 81.2 %copy-start.55 = (f32[8,128]{1,0:T(8,128)}, f32[8,128]{1,0:T(8,128)S(1)}, u32[]{:S(2)}) copy-start(f32[8,128]{1,0:T(8,128)S(1)} %copy.108) | copy-start | bytes 12292
  110.9 81.2 %copy-start.65 = (f32[8,128]{1,0:T(8,128)}, f32[8,128]{1,0:T(8,128)S(1)}, u32[]{:S(2)}) copy-start(f32[8,128]{1,0:T(8,128)S(1)} %copy.109) | copy-start | bytes 12292
  110.9 81.1 %copy-start.61 = (f32[8,128]{1,0:T(8,128)}, f32[8,128]{1,0:T(8,128)S(1)}, u32[]{:S(2)}) copy-start(f32[8,128]{1,0:T(8,128)S(1)} %copy.110) | copy-start | bytes 12292
  111.0 81.0 %copy-start.59 = (f32[8,128]{1,0:T(8,128)}, f32[8,128]{1,0:T(8,128)S(1)}, u32[]{:S(2)}) copy-start(f32[8,128]{1,0:T(8,128)S(1)} %copy.111) | copy-start | bytes 12292
  111.1 81.0 %copy-start.53 = (f32[8,128]{1,0:T(8,128)}, f32[8,128]{1,0:T(8,128)S(1)}, u32[]{:S(2)}) copy-start(f32[8,128]{1,0:T(8,128)S(1)} %copy.104) | copy-start | bytes 12292
  111.2 80.9 %copy-start.71 = (f32[8,128]{1,0:T(8,128)}, f32[8,128]{1,0:T(8,128)S(1)}, u32[]{:S(2)}) copy-start(f32[8,128]{1,0:T(8,128)S(1)} %copy.105) | copy-start | bytes 12292
  111.2 80.8 %copy-start.67 = (f32[8,128]{1,0:T(8,128)}, f32[8,128]{1,0:T(8,128)S(1)}, u32[]{:S(2)}) copy-start(f32[8,128]{1,0:T(8,128)S(1)} %copy.106) | copy-start | bytes 12292
  111.7 537.5 %copy-start.46 = (f32[512]{0:T(512)}, f32[512]{0:T(512)S(1)}, u32[]{:S(2)}) copy-start(f32[512]{0:T(512)S(1)} %get-tuple-element.697) | copy-start | bytes 6148
  111.7 538.1 %copy-start.48 = (f32[512]{0:T(512)}, f32[512]{0:T(512)S(1)}, u32[]{:S(2)}) copy-start(f32[512]{0:T(512)S(1)} %get-tuple-element.698) | copy-start | bytes 6148
  111.7 538.8 %copy-start.50 = (f32[512]{0:T(512)}, f32[512]{0:T(512)S(1)}, u32[]{:S(2)}) copy-start(f32[512]{0:T(512)S(1)} %get-tuple-element.699) | copy-start | bytes 6148
  645.3 280.9 %all-gather.7.cloned.1.call-start = ((), (), s32[]{:S(2)}) async-start(), calls=%async_computation.5 | async-start | bytes 36765696 | tf_op jit(solution)/shard_map/all_gather | solution.py:141
  649.2 393.9 %all-reduce.52.cloned.1.call-start = ((), (), s32[]{:S(2)}) async-start(), calls=%async_computation.6 | async-start | bytes 4194304 | tf_op jit(solution)/shard_map/psum | solution.py:216
  669.5 378.5 %copy-start.41 = (f32[16,1,128]{2,1,0:T(1,128)}, f32[16,1,128]{2,1,0:T(1,128)S(1)}, u32[]{:S(2)}) copy-start(f32[16,1,128]{2,1,0:T(1,128)S(1)} %convert_element_type.233) | copy-start | bytes 24580
  756.2 291.7 %copy-start.80 = (f32[512]{0:T(512)}, f32[512]{0:T(512)S(1)}, u32[]{:S(2)}) copy-start(f32[512]{0:T(512)S(1)} %fusion.175) | copy-start | bytes 6148
  980.0 762.4 %all-reduce.54.cloned.1.call-start = ((), (), s32[]{:S(2)}) async-start(), calls=%async_computation.10 | async-start | bytes 8388608 | tf_op jit(solution)/shard_map/psum | solution.py:185
  1062.7 495.6 %copy-start.44 = (f32[512,8]{0,1:T(8,128)S(1)}, f32[512,8]{0,1:T(8,128)}, u32[]{:S(2)}) copy-start(f32[512,8]{0,1:T(8,128)} %copy-done.43) | copy-start | bytes 49156
  1062.7 500.5 %copy-start.36 = (f32[512,8]{0,1:T(8,128)S(1)}, f32[512,8]{0,1:T(8,128)}, u32[]{:S(2)}) copy-start(f32[512,8]{0,1:T(8,128)} %copy-done.35) | copy-start | bytes 49156
  1598.1 446.4 %reduce-scatter.5.cloned.1.call-start = ((), (), s32[]{:S(2)}) async-start(), calls=%async_computation.7 | async-start | bytes 35651584 | tf_op jit(solution)/shard_map/reduce_scatter | solution.py:235
  1643.4 456.4 %reduce-scatter.7.cloned.1.call-start = ((), (), s32[]{:S(2)}) async-start(), calls=%async_computation.8 | async-start | bytes 69632 | tf_op jit(solution)/shard_map/reduce_scatter | solution.py:257
  1686.3 1072.9 %reduce-scatter.9.cloned.1.call-start = ((), (), s32[]{:S(2)}) async-start(), calls=%async_computation.9 | async-start | bytes 73531392 | tf_op jit(solution)/shard_map/reduce_scatter | solution.py:207
  (89 other events, 1111.6 us)
Sparse Core Ops, SparseCore 0:
  11.3 134.1 all-gather.4
  645.4 106.0 all-reduce.49
  753.2 172.9 all-gather.6
  980.1 62.9 all-reduce.51
  1598.2 108.2 all-reduce.53
  1711.2 333.2 reduce-scatter.4
  2048.8 50.9 reduce-scatter.6
  2104.6 654.5 reduce-scatter.8
where the time goes:
time: 2770 us
  waiting for transfers between devices  1250 us (45%)
  other arithmetic  788 us (28%)
  matrix products  384 us (14%)
  blocking collectives  181 us (7%)
  local copies, waits for them, and re-layouts  140 us (5%)
    reduce_scatter x2, waiting for transfers between devices, body(): lax.psum_scatter(jnp.concatenate([first_part, last_part[:, None]], axis=1...  883 us
    another operation x64, other arithmetic, delta_block(): lax.linalg.triangular_solve(system, target, left_side=True, lower=True, u...  632 us
    all_gather x1, waiting for transfers between devices, body(): lax.all_gather(mlp_low, 'dp', axis=0, tiled=True)  170 us
    unnamed x2, blocking collectives  99.7 us
    concatenate x2, other arithmetic, body(): jnp.concatenate([first_part, last_part[:, None]], axis=1)  69.9 us
    psum x1, waiting for transfers between devices, body(): attended = lax.psum(attn_part, 'tensor')  67.2 us
  transfers between devices with their start and end apart: 8, of which 7 were waited for; matrix products, arithmetic and copies ran while one was open for 7% of the time, Pallas kernels for 0%

commit v1 on v0

--- a/solution.py
+++ b/solution.py
@@ -5,6 +5,29 @@
 
 BLOCK = 64
 highest = lax.Precision.HIGHEST
+
+
+def laid_out(blocks, dim):
+    blocks = jnp.moveaxis(blocks, 0, dim)
+    shape = blocks.shape
+    return blocks.reshape(*shape[:dim], shape[dim] * shape[dim + 1], *shape[dim + 2 :])
+
+
+def grow_blocks(x, axis):
+    size, mine = (lax.axis_size(axis), lax.axis_index(axis))
+    blocks, bit = (x[None], 1)
+    while bit < size:
+        partner_block = lax.ppermute(blocks, axis, [(i, i ^ bit) for i in range(size)])
+        low = mine & bit == 0
+        blocks = jnp.concatenate(
+            [jnp.where(low, blocks, partner_block), jnp.where(low, partner_block, blocks)]
+        )
+        bit *= 2
+    return blocks
+
+
+def collect(x, axis, dim):
+    return laid_out(grow_blocks(x, axis), dim)
 
 
 def rms_scale(values, gain_values, epsilon):
@@ -138,7 +161,7 @@
     )
     gain_mid, mlp_mat = (
         lax.all_gather(gain_mid_low, "dp", axis=0, tiled=True),
-        lax.all_gather(mlp_low, "dp", axis=0, tiled=True),
+        collect(mlp_low, "dp", 0),
     )
     model_width = attn_mat.shape[0]
     local_width = attn_mat.shape[2]

time: 2770 us -> 3880 us (1.40)
  waiting for transfers between devices: 1250 us -> 1810 us
  blocking collectives: 181 us -> 547 us
  other arithmetic: 788 us -> 906 us
  local copies, waits for them, and re-layouts: 140 us -> 188 us
    ppermute x0 -> x4, waiting for transfers between devices: none -> 773 us  [grow_blocks(): lax.ppermute(blocks, axis, [(i, i ^ bit) for i in range(size)])]
    all_gather x1, blocking collectives: 18.3 us -> 384 us  [body(): lax.all_gather(gain_mid_low, 'dp', axis=0, tiled=True)]
    all_gather x1, waiting for transfers between devices: 170 us -> 0.01 us  [body(): lax.all_gather(mlp_low, 'dp', axis=0, tiled=True)]
    psum x1, waiting for transfers between devices: 67.2 us -> 0.01 us  [body(): attended = lax.psum(attn_part, 'tensor')]
    concatenate x0 -> x4, other arithmetic: none -> 44.4 us  [grow_blocks(): jnp.concatenate([jnp.where(low, blocks, partner_block), jnp.where(low, pa...]
    select_n x0 -> x4, other arithmetic: none -> 39.6 us  [grow_blocks(): jnp.where(low, blocks, partner_block)]
  transfers between devices with their start and end apart: 8 -> 12, of which waited for: 7 -> 9; matrix products, arithmetic and copies ran while one was open for 7% -> 9% of each run, Pallas kernels for 0% -> 0%
where the time goes in v1:
time: 3880 us; the launch traced here: 3870 us
  waiting for transfers between devices  1810 us (47%)
  other arithmetic  906 us (23%)
  blocking collectives  547 us (14%)
  matrix products  395 us (10%)
  local copies, waits for them, and re-layouts  188 us (5%)
    reduce_scatter x2, waiting for transfers between devices, body(): lax.psum_scatter(jnp.concatenate([first_part, last_part[:, None]], axis=1...  883 us
    ppermute x4, waiting for transfers between devices, grow_blocks(): lax.ppermute(blocks, axis, [(i, i ^ bit) for i in range(size)])  773 us
    another operation x64, other arithmetic, delta_block(): lax.linalg.triangular_solve(system, target, left_side=True, lower=True, u...  649 us
    all_gather x1, blocking collectives, body(): lax.all_gather(gain_mid_low, 'dp', axis=0, tiled=True)  384 us
    unnamed x2, blocking collectives  95.2 us
  transfers between devices with their start and end apart: 12, of which 9 were waited for; matrix products, arithmetic and copies ran while one was open for 9% of the time, Pallas kernels for 0%

profile of v1, /device:TPU:0, one launch (start us, length us, event | category | flops | bytes accessed | tf_op | source)
XLA Modules:
  0.0 3872.8 jit_solution(2989332917904533534)
XLA Ops:
  199.3 455.4 %while.38 = (s32[]{:T(128)}, f32[8,128,128]{2,1,0:T(8,128)S(1)}, f32[8,64,8,128]{3,1,2,0:T(8,128)}, f32[8,8,128,128]{3,2,1,0:T(8,128)}, s32[8,64]{1,0:T(8,128)},...) while((s32[]{:T(128)}, f32[8,128,128]{2,1,0:T(8,128)S(1)}, ...), condition=%wide.region_4.6_spmd.clone, body=%wide.region_3.5_spmd.clone.sunk | while | flops 504746240 | bytes 7759869 | solution.py:104
  210.0 40.0 %custom-call.24 = f32[8,1,64,64]{2,3,1,0:T(8,128)S(1)} custom-call(f32[8,1,64,64]{3,2,1,0:T(8,128)} %fusion.307), custom_call_target="InvertDiagBlocksLowerTriangular" | custom-call | tf_op jit(solution)/shard_map/jvp()/while/body/eval_jaxpr/triangular_solve/custom-call.1 | solution.py:76
  266.8 40.0 %custom-call.24 = f32[8,1,64,64]{2,3,1,0:T(8,128)S(1)} custom-call(f32[8,1,64,64]{3,2,1,0:T(8,128)} %fusion.307), custom_call_target="InvertDiagBlocksLowerTriangular" | custom-call | tf_op jit(solution)/shard_map/jvp()/while/body/eval_jaxpr/triangular_solve/custom-call.1 | solution.py:76
  323.7 40.0 %custom-call.24 = f32[8,1,64,64]{2,3,1,0:T(8,128)S(1)} custom-call(f32[8,1,64,64]{3,2,1,0:T(8,128)} %fusion.307), custom_call_target="InvertDiagBlocksLowerTriangular" | custom-call | tf_op jit(solution)/shard_map/jvp()/while/body/eval_jaxpr/triangular_solve/custom-call.1 | solution.py:76
  380.6 40.0 %custom-call.24 = f32[8,1,64,64]{2,3,1,0:T(8,128)S(1)} custom-call(f32[8,1,64,64]{3,2,1,0:T(8,128)} %fusion.307), custom_call_target="InvertDiagBlocksLowerTriangular" | custom-call | tf_op jit(solution)/shard_map/jvp()/while/body/eval_jaxpr/triangular_solve/custom-call.1 | solution.py:76
  494.3 40.0 %custom-call.24 = f32[8,1,64,64]{2,3,1,0:T(8,128)S(1)} custom-call(f32[8,1,64,64]{3,2,1,0:T(8,128)} %fusion.307), custom_call_target="InvertDiagBlocksLowerTriangular" | custom-call | tf_op jit(solution)/shard_map/jvp()/while/body/eval_jaxpr/triangular_solve/custom-call.1 | solution.py:76
  551.1 40.0 %custom-call.24 = f32[8,1,64,64]{2,3,1,0:T(8,128)S(1)} custom-call(f32[8,1,64,64]{3,2,1,0:T(8,128)} %fusion.307), custom_call_target="InvertDiagBlocksLowerTriangular" | custom-call | tf_op jit(solution)/shard_map/jvp()/while/body/eval_jaxpr/triangular_solve/custom-call.1 | solution.py:76
  608.0 40.0 %custom-call.24 = f32[8,1,64,64]{2,3,1,0:T(8,128)S(1)} custom-call(f32[8,1,64,64]{3,2,1,0:T(8,128)} %fusion.307), custom_call_target="InvertDiagBlocksLowerTriangular" | custom-call | tf_op jit(solution)/shard_map/jvp()/while/body/eval_jaxpr/triangular_solve/custom-call.1 | solution.py:76
  685.9 94.4 %collective-permute-done.1 = bf16[2,128,3,2816]{3,1,2,0:T(8,128)(2,1)} collective-permute-done((bf16[2,128,3,2816]{3,1,2,0:T(8,128)(2,1)}, bf16[2,128,3,2816]{3,1,2,0:T(8,128)(2,1)}, u32[]{:S(2)}, u32[]{:S(2)}) %collective-permute-start.1) | collective-permute-done | bytes 4325408 | tf_op jit(solution)/shard_map/ppermute | solution.py:20
  796.3 333.4 %collective-permute-done.2 = bf16[4,128,3,2816]{3,1,2,0:T(8,128)(2,1)} collective-permute-done((bf16[4,128,3,2816]{3,1,2,0:T(8,128)(2,1)}, bf16[4,128,3,2816]{3,1,2,0:T(8,128)(2,1)}, u32[]{:S(2)}, u32[]{:S(2)}) %collective-permute-start.2) | collective-permute-done | bytes 8650784 | tf_op jit(solution)/shard_map/ppermute | solution.py:20
  1151.8 384.4 %all-gather.1 = bf16[16,1,128]{2,1,0:T(2,128)(2,1)S(1)} all-gather(bf16[1,1,128]{2,1,0:T(2,128)(2,1)S(1)} %convert_bitcast_fusion.1), channel_id=1, replica_groups=mesh['dp'=16,'tensor'=2] {'dp'}, dimensions={0}, use_global_device_ids=true | all-gather | bytes 4352 | tf_op jit(solution)/shard_map/all_gather | solution.py:163
  1551.2 341.3 %collective-permute-done.3 = bf16[8,128,3,2816]{3,1,2,0:T(8,128)(2,1)} collective-permute-done((bf16[8,128,3,2816]{3,1,2,0:T(8,128)(2,1)}, bf16[8,128,3,2816]{3,1,2,0:T(8,128)(2,1)}, u32[]{:S(2)}, u32[]{:S(2)}) %collective-permute-start.3) | collective-permute-done | bytes 17301536 | tf_op jit(solution)/shard_map/ppermute | solution.py:20
  2037.4 71.6 %all-reduce.52.cloned.1.call-done = bf16[512,2048]{1,0:T(8,128)(2,1)} async-done(((bf16[512,2048]{1,0:T(8,128)(2,1)}), bf16[512,2048]{1,0:T(8,128)(2,1)}) %all-reduce.52.cloned.1.call-update) | async-done | bytes 2097168 | tf_op jit(solution)/shard_map/psum | solution.py:239
  2128.6 536.0 %while.39 = (s32[]{:T(128)}, f32[8,128,128]{2,1,0:T(8,128)}, f32[8,64,8,128]{3,1,0,2:T(8,128)}, f32[8,64,8,128]{3,1,0,2:T(8,128)}, f32[8,64,8,128]{3,1,0,2:T(8,1...) while((s32[]{:T(128)}, f32[8,128,128]{2,1,0:T(8,128)}, ...), condition=%wide.region_15.17_spmd.clone, body=%wide.region_12.16_spmd.clone.sunk | while | flops 1285967616 | bytes 23185976 | solution.py:104
  2209.6 40.0 %custom-call.25 = f32[8,1,64,64]{2,3,1,0:T(8,128)S(1)} custom-call(f32[8,1,64,64]{3,2,1,0:T(8,128)} %add_bitcast_fusion.8), custom_call_target="InvertDiagBlocksLowerTriangular" | custom-call | tf_op jit(solution)/shard_map/transpose(jvp())/while/body/eval_jaxpr/checkpoint/triangular_solve | solution.py:76
  2276.7 40.0 %custom-call.25 = f32[8,1,64,64]{2,3,1,0:T(8,128)S(1)} custom-call(f32[8,1,64,64]{3,2,1,0:T(8,128)} %add_bitcast_fusion.8), custom_call_target="InvertDiagBlocksLowerTriangular" | custom-call | tf_op jit(solution)/shard_map/transpose(jvp())/while/body/eval_jaxpr/checkpoint/triangular_solve | solution.py:76
  2343.8 40.0 %custom-call.25 = f32[8,1,64,64]{2,3,1,0:T(8,128)S(1)} custom-call(f32[8,1,64,64]{3,2,1,0:T(8,128)} %add_bitcast_fusion.8), custom_call_target="InvertDiagBlocksLowerTriangular" | custom-call | tf_op jit(solution)/shard_map/transpose(jvp())/while/body/eval_jaxpr/checkpoint/triangular_solve | solution.py:76
  2410.8 40.0 %custom-call.25 = f32[8,1,64,64]{2,3,1,0:T(8,128)S(1)} custom-call(f32[8,1,64,64]{3,2,1,0:T(8,128)} %add_bitcast_fusion.8), custom_call_target="InvertDiagBlocksLowerTriangular" | custom-call | tf_op jit(solution)/shard_map/transpose(jvp())/while/body/eval_jaxpr/checkpoint/triangular_solve | solution.py:76
  2612.2 40.0 %custom-call.25 = f32[8,1,64,64]{2,3,1,0:T(8,128)S(1)} custom-call(f32[8,1,64,64]{3,2,1,0:T(8,128)} %add_bitcast_fusion.8), custom_call_target="InvertDiagBlocksLowerTriangular" | custom-call | tf_op jit(solution)/shard_map/transpose(jvp())/while/body/eval_jaxpr/checkpoint/triangular_solve | solution.py:76
  2793.2 49.1 %pad_maximum_fusion = f32[2048,3,2816]{2,0,1:T(8,128)} fusion(f32[2048,1,2816]{2,0,1:T(8,128)} %convolution_bitcast_fusion.5, f32[2048,2,2816]{2,0,1:T(8,128)} %fusion.116), kind=kLoop, calls=%fused_computation.142 | loop fusion | flops 17301504 | bytes 138412032 | tf_op jit(solution)/shard_map/concatenate | solution.py:231
  2852.8 63.7 %all-reduce.55 = (f32[2048]{0:T(1024)S(1)}, f32[3,4,8,128]{3,2,1,0:T(8,128)S(1)}, f32[128]{0:T(128)S(1)}, f32[2048]{0:T(1024)S(1)}) all-reduce(f32[2048]{0:T(1024)S(1)} %get-tuple-element.569, f32[3,4,8,128]{3,2,1,0:T(8,128)S(1)} %pad_add_fusion, bf16[128]{0:T(256)(128)(2,1)S(1)} %psum.39, ...), channel_id=2, replica_groups=mesh['dp'=16,'tensor'=2] {'dp'}, use_global_device_ids=true, to_apply=%region_21.23.clone | all-reduce | flops 16512 | bytes 131840
  2927.2 224.1 %reduce-scatter.5.cloned.1.call-done = f32[128,4,1024]{2,0,1:T(8,128)} async-done(((f32[2048,4,1024]{2,0,1:T(8,128)}), f32[128,4,1024]{2,0,1:T(8,128)}) %reduce-scatter.5.cloned.1.call-update) | async-done | bytes 2097168 | tf_op jit(solution)/shard_map/reduce_scatter | solution.py:258
  3155.5 50.9 %reduce-scatter.7.cloned.1.call-done = f32[128,8]{0,1:T(8,128)} async-done(((f32[2048,8]{0,1:T(8,128)}), f32[128,8]{0,1:T(8,128)}) %reduce-scatter.7.cloned.1.call-update) | async-done | bytes 4112 | tf_op jit(solution)/shard_map/reduce_scatter | solution.py:280
  3206.4 659.3 %reduce-scatter.9.cloned.1.call-done = f32[128,3,2816]{2,0,1:T(8,128)} async-done(((f32[2048,3,2816]{2,0,1:T(8,128)}), f32[128,3,2816]{2,0,1:T(8,128)}) %reduce-scatter.9.cloned.1.call-update) | async-done | bytes 4325392 | tf_op jit(solution)/shard_map/reduce_scatter | solution.py:230
  (889 shorter events, 1098.9 us)
Async XLA Ops:
  7.2 135.6 %all-gather.5.cloned.1.call-start = ((), (), s32[]{:S(2)}) async-start(), calls=%async_computation.3 | async-start | bytes 17825792 | tf_op jit(solution)/shard_map/all_gather | solution.py:157
  11.1 1952.3 %all-reduce.50.cloned.1.call-start = ((), (), s32[]{:S(2)}) async-start(), calls=%async_computation.4 | async-start | bytes 8388608 | tf_op jit(solution)/shard_map/psum | solution.py:196
  36.3 134.1 %copy-start.47 = (f32[16,1,128]{2,1,0:T(1,128)}, f32[16,1,128]{2,1,0:T(1,128)S(1)}, u32[]{:S(2)}) copy-start(f32[16,1,128]{2,1,0:T(1,128)S(1)} %convert_element_type.232) | copy-start | bytes 24580
  54.9 115.5 %copy-start.88 = (f32[512]{0:T(512)}, f32[512]{0:T(512)S(1)}, u32[]{:S(2)}) copy-start(f32[512]{0:T(512)S(1)} %fusion.174) | copy-start | bytes 6148
  78.3 111.1 %copy-start.69 = (f32[8,128]{1,0:T(8,128)}, f32[8,128]{1,0:T(8,128)S(1)}, u32[]{:S(2)}) copy-start(f32[8,128]{1,0:T(8,128)S(1)} %copy.113) | copy-start | bytes 12292
  78.4 111.1 %copy-start.77 = (f32[8,128]{1,0:T(8,128)}, f32[8,128]{1,0:T(8,128)S(1)}, u32[]{:S(2)}) copy-start(f32[8,128]{1,0:T(8,128)S(1)} %copy.112) | copy-start | bytes 12292
  78.5 111.0 %copy-start.83 = (f32[8,128]{1,0:T(8,128)}, f32[8,128]{1,0:T(8,128)S(1)}, u32[]{:S(2)}) copy-start(f32[8,128]{1,0:T(8,128)S(1)} %copy.111) | copy-start | bytes 12292
  111.9 545.2 %copy-start.109 = (f32[128]{0:T(128)}, f32[128]{0:T(128)S(1)}, u32[]{:S(2)}) copy-start(f32[128]{0:T(128)S(1)} %convert_element_type.207) | copy-start | bytes 1540
  112.5 1037.2 %copy-start.56 = (f32[512]{0:T(512)}, f32[512]{0:T(512)S(1)}, u32[]{:S(2)}) copy-start(f32[512]{0:T(512)S(1)} %get-tuple-element.705) | copy-start | bytes 6148
  112.5 1037.9 %copy-start.60 = (f32[512]{0:T(512)}, f32[512]{0:T(512)S(1)}, u32[]{:S(2)}) copy-start(f32[512]{0:T(512)S(1)} %get-tuple-element.707) | copy-start | bytes 6148
  112.5 1038.6 %copy-start.58 = (f32[512]{0:T(512)}, f32[512]{0:T(512)S(1)}, u32[]{:S(2)}) copy-start(f32[512]{0:T(512)S(1)} %get-tuple-element.706) | copy-start | bytes 6148
  665.1 1323.5 %all-gather.7.cloned.1.call-start = ((), (), s32[]{:S(2)}) async-start(), calls=%async_computation.5 | async-start | bytes 36765696 | tf_op jit(solution)/shard_map/all_gather | solution.py:217
  669.0 1440.0 %all-reduce.52.cloned.1.call-start = ((), (), s32[]{:S(2)}) async-start(), calls=%async_computation.6 | async-start | bytes 4194304 | tf_op jit(solution)/shard_map/psum | solution.py:239
  673.1 4.6 collective-permute-start
  684.6 95.7 %collective-permute-start.1 = (bf16[2,128,3,2816]{3,1,2,0:T(8,128)(2,1)}, bf16[2,128,3,2816]{3,1,2,0:T(8,128)(2,1)}, u32[]{:S(2)}, u32[]{:S(2)}) collective-permute-start(bf16[2,128,3,2816]{3,1,2,0:T(8,128)(2,1)} %pad_maximum_fusion.6), channel_id=1, source_target_pairs={{0,4},{2,6},{4,0},{6,2},{8,12},{10,14},{12,8},{14,10},{16,20},{18,... | collective-permute-start | bytes 12976136 | tf_op jit(solution)/shard_map/ppermute | solution.py:20
  794.7 335.0 %collective-permute-start.2 = (bf16[4,128,3,2816]{3,1,2,0:T(8,128)(2,1)}, bf16[4,128,3,2816]{3,1,2,0:T(8,128)(2,1)}, u32[]{:S(2)}, u32[]{:S(2)}) collective-permute-start(bf16[4,128,3,2816]{3,1,2,0:T(8,128)(2,1)} %pad_maximum_fusion.4), channel_id=1, source_target_pairs={{0,8},{2,10},{4,12},{6,14},{8,0},{10,2},{12,4},{14,6},{16,24},{18,... | collective-permute-start | bytes 25952264 | tf_op jit(solution)/shard_map/ppermute | solution.py:20
  1147.4 745.2 %collective-permute-start.3 = (bf16[8,128,3,2816]{3,1,2,0:T(8,128)(2,1)}, bf16[8,128,3,2816]{3,1,2,0:T(8,128)(2,1)}, u32[]{:S(2)}, u32[]{:S(2)}) collective-permute-start(bf16[8,128,3,2816]{3,1,2,0:T(8,128)(2,1)} %pad_maximum_fusion.3), channel_id=1, source_target_pairs={{0,16},{2,18},{4,20},{6,22},{8,24},{10,26},{12,28},{14,30},{16,0},... | collective-permute-start | bytes 51904520 | tf_op jit(solution)/shard_map/ppermute | solution.py:20
  1536.2 577.7 %copy-start.49 = (f32[16,1,128]{2,1,0:T(1,128)}, f32[16,1,128]{2,1,0:T(1,128)S(1)}, u32[]{:S(2)}) copy-start(f32[16,1,128]{2,1,0:T(1,128)S(1)} %convert_element_type.233) | copy-start | bytes 24580
  1968.1 145.9 %copy-start.90 = (f32[512]{0:T(512)}, f32[512]{0:T(512)S(1)}, u32[]{:S(2)}) copy-start(f32[512]{0:T(512)S(1)} %fusion.175) | copy-start | bytes 6148
  2022.3 826.8 %all-reduce.54.cloned.1.call-start = ((), (), s32[]{:S(2)}) async-start(), calls=%async_computation.10 | async-start | bytes 8388608 | tf_op jit(solution)/shard_map/psum | solution.py:208
  2128.6 541.0 %copy-start.40 = (f32[512,8]{0,1:T(8,128)S(1)}, f32[512,8]{0,1:T(8,128)}, u32[]{:S(2)}) copy-start(f32[512,8]{0,1:T(8,128)} %copy-done.39) | copy-start | bytes 49156
  2704.9 446.3 %reduce-scatter.5.cloned.1.call-start = ((), (), s32[]{:S(2)}) async-start(), calls=%async_computation.7 | async-start | bytes 35651584 | tf_op jit(solution)/shard_map/reduce_scatter | solution.py:258
  2750.3 456.1 %reduce-scatter.7.cloned.1.call-start = ((), (), s32[]{:S(2)}) async-start(), calls=%async_computation.8 | async-start | bytes 69632 | tf_op jit(solution)/shard_map/reduce_scatter | solution.py:280
  2793.1 1072.6 %reduce-scatter.9.cloned.1.call-start = ((), (), s32[]{:S(2)}) async-start(), calls=%async_computation.9 | async-start | bytes 73531392 | tf_op jit(solution)/shard_map/reduce_scatter | solution.py:230
  (120 other events, 1673.0 us)
Sparse Core Ops, SparseCore 0:
  11.2 131.5 all-gather.4
  665.2 106.4 all-reduce.49
  773.4 319.1 all-gather.6
  2022.4 86.5 all-reduce.51
  2705.0 108.2 all-reduce.53
  2818.0 333.2 reduce-scatter.4
  3155.5 50.8 reduce-scatter.6
  3211.2 654.4 reduce-scatter.8
